TPU v7x, 256 devices: a whole 4x4x8 slice. The times are simulated.
256 devices in a mesh: seq: 16 (over x_hi, y, core), heads: 16 (over z, x_lo).
Axes of the slice: x: 4 (x_hi: 2, x_lo: 2; x = x_hi * 2 + x_lo), y: 4, z: 8, core: 2. Of those that a mesh axis runs over, the one named last changes fastest.
Arguments:
- activations: bfloat16 [12288, 4096], P('seq', 'heads'), may hold values from -24 to 24
- w_query: bfloat16 [4096, 4096], P(None, 'heads'), may hold values from -0.1875 to 0.1875
- w_key: bfloat16 [4096, 4096], P(None, 'heads'), may hold values from -0.09375 to 0.09375
- w_value: bfloat16 [4096, 4096], P(None, 'heads'), may hold values from -0.09375 to 0.09375
- w_out: bfloat16 [4096, 4096], P('heads'), may hold values from -0.1875 to 0.1875
- windows: int32 [32], P('heads'), may hold values from 1 to 2, as said below
- rand_blocks: int32 [96, 3], P('seq'), may hold values from 0 to 95, as said below
- global_pos: int32 [128], replicated, may hold values from 0 to 12287, as said below
Outputs:
- attended: bfloat16 [12288, 4096], P('seq', 'heads')
Inputs may be any that keep to these rules, and one draw needn't show every extreme that they name: `windows`: some head has reach 2. `rand_blocks`: the 3 entries of a row are distinct. Of the 18 entries in the rows of one index of seq, at most 2 fall into the 6 blocks of any one index, and exactly 2 into those of some index. `global_pos`: Distinct. At most 32 fall into the 768 positions of one index of seq, and exactly 32 into those of some index.
All inputs are finite; a program needn't handle non-finite values.
Results may differ from a plain program's by a relative error of at most 0.024.
The roundings to bfloat16 on the way count: a program that leaves them out, or rounds other values in their place, can miss the bound.
Values may be sent and summed in bfloat16 or wider, within the bound.
No kernel may reach another device: no remote copies, remote signals or barrier semaphores. Data moves between devices by JAX's collectives and lax.ppermute only.
A program may use at most 128 MiB of HBM per device.

v0:
```python
import math
import jax
import jax.numpy as jnp
from jax import lax
from jax.sharding import PartitionSpec as P

WMAX = 2
NEGATIVE = -1e30


def extended(block, sides, width):
    for axis, dim in sides:
        count = lax.axis_size(axis)
        forward = [(i, i + 1) for i in range(count - 1)]
        forward.append((count - 1, 0))
        backward = [(target, source) for source, target in forward]
        low = lax.ppermute(
            lax.slice_in_dim(block, block.shape[dim] - width, None, axis=dim), axis, forward
        )
        high = lax.ppermute(lax.slice_in_dim(block, 0, width, axis=dim), axis, backward)
        block = jnp.concatenate([low, block, high], axis=dim)
    return block


def combined_all(value, axis, join):
    pieces = jax.tree.map(lambda part: lax.all_gather(part, axis), value)
    head = jax.tree.map(lambda part: part[0], pieces)
    tail = jax.tree.map(lambda part: part[1:], pieces)
    running, _ = lax.scan(lambda running, slab: (join(running, slab), None), head, tail)
    return running


def fold_scores(state, scores, valid):
    top_old, sum_old, acc_old = state
    masked = jnp.where(valid, scores, NEGATIVE)
    top_new = jnp.maximum(top_old, jnp.max(masked, axis=-1))
    probs = jnp.where(valid, jnp.exp(masked - top_new[..., None]), 0.0)
    keep = jnp.exp(top_old - top_new)
    return (
        top_new,
        keep * sum_old + jnp.sum(probs, axis=-1),
        keep[..., None] * acc_old,
        probs.astype(jnp.bfloat16),
    )


def join_states(first, second):
    top_first, sum_first, acc_first = first
    top_second, sum_second, acc_second = second
    top_both = jnp.maximum(top_first, top_second)
    keep_first = jnp.exp(top_first - top_both)
    keep_second = jnp.exp(top_second - top_both)
    return (
        top_both,
        keep_first * sum_first + keep_second * sum_second,
        keep_first[..., None] * acc_first + keep_second[..., None] * acc_second,
    )


def on_device(activations, w_query, w_key, w_value, w_out, windows, rand_blocks, global_pos):
    rows_here = activations.shape[0]
    group_width = w_query.shape[1]
    heads_here = windows.shape[0]
    head_size = group_width // heads_here
    blocks_here = rand_blocks.shape[0]
    block_rows = rows_here // blocks_here
    picks_per_block = rand_blocks.shape[1]
    seq_count = lax.axis_size("seq")
    position = lax.axis_index("seq")
    score_scale = 1.0 / math.sqrt(head_size)
    piece = lax.all_gather(activations, "heads", axis=1, tiled=True)
    sums_query = jnp.dot(piece, w_query, preferred_element_type=jnp.float32)
    sums_key = jnp.dot(piece, w_key, preferred_element_type=jnp.float32)
    sums_value = jnp.dot(piece, w_value, preferred_element_type=jnp.float32)
    query = sums_query.astype(jnp.bfloat16)
    keys = sums_key.astype(jnp.bfloat16)
    values = sums_value.astype(jnp.bfloat16)
    query_blocks = query.reshape(blocks_here, block_rows, heads_here, head_size)
    stacked = jnp.stack([keys, values], 0)
    padded = extended(stacked, (("seq", 1),), WMAX * block_rows)
    span = 2 * WMAX + 1
    padded_blocks = padded.reshape(2, blocks_here + 2 * WMAX, block_rows, heads_here, head_size)
    window_kv = jnp.concatenate(
        [padded_blocks[:, offset : offset + blocks_here, None] for offset in range(span)], axis=2
    )
    window_kv = window_kv.reshape(2, blocks_here, span * block_rows, heads_here, head_size)
    distance = jnp.abs(jnp.arange(span, dtype=jnp.int32) - WMAX)
    window_valid = jnp.repeat(distance[None, :] <= windows[:, None], block_rows, axis=1)[
        None, :, None, :
    ]
    scores = (
        jnp.einsum(
            "bqhd,bkhd->bhqk", query_blocks, window_kv[0], preferred_element_type=jnp.float32
        )
        * score_scale
    )
    start_state = (
        jnp.full((blocks_here, heads_here, block_rows), NEGATIVE, jnp.float32),
        jnp.zeros((blocks_here, heads_here, block_rows), jnp.float32),
        jnp.zeros((blocks_here, heads_here, block_rows, head_size), jnp.float32),
    )
    top, total, accum, attention_weights = fold_scores(start_state, scores, window_valid)
    accum = jnp.einsum(
        "bhqk,bkhd->bhqd", attention_weights, window_kv[1], preferred_element_type=jnp.float32
    )
    state = (top, total, accum)
    all_valid = jnp.ones((1, 1, 1, 1), dtype=bool)
    targets = rand_blocks.reshape(-1)
    request_count = targets.shape[0]
    sources = targets // blocks_here
    order = jnp.arange(request_count, dtype=jnp.int32)
    earlier = (sources[:, None] == sources[None, :]) & (order[None, :] < order[:, None])
    ranks = jnp.sum(earlier.astype(jnp.int32), axis=1)
    slot_count = (request_count + seq_count - 1) // seq_count
    hits = (sources[:, None, None] == jnp.arange(seq_count, dtype=jnp.int32)[None, :, None]) & (
        ranks[:, None, None] == jnp.arange(slot_count, dtype=jnp.int32)[None, None, :]
    )
    slot_request = jnp.sum(jnp.where(hits, order[:, None, None], 0), axis=0)
    slot_live = jnp.any(hits, axis=0)
    row_steps = jnp.arange(block_rows, dtype=jnp.int32)
    owner_ids = jnp.arange(blocks_here, dtype=jnp.int32)
    piece = lax.all_gather(stacked, "seq", axis=1, tiled=True)
    count = piece.shape[1]
    picked = slot_request.reshape(-1)
    alive = slot_live.reshape(-1)
    slot_total = picked.shape[0]
    offset_rows = targets[picked][:, None] * block_rows + row_steps[None, :]
    chosen = piece[:, jnp.clip(offset_rows, 0, count - 1).reshape(-1)]
    chosen = chosen.reshape(2, slot_total * block_rows, heads_here, head_size)
    part_scores = (
        jnp.einsum("bqhd,khd->bhqk", query_blocks, chosen[0], preferred_element_type=jnp.float32)
        * score_scale
    )
    belongs = alive[None, :] & ((picked // picks_per_block)[None, :] == owner_ids[:, None])
    valid = jnp.repeat(belongs, block_rows, axis=1)[:, None, None, :]
    top_new, total_new, accum_new, part_weights = fold_scores(state, part_scores, valid)
    state = (
        top_new,
        total_new,
        accum_new
        + jnp.einsum("bhqk,khd->bhqd", part_weights, chosen[1], preferred_element_type=jnp.float32),
    )
    global_count = global_pos.shape[0]
    local_pos = global_pos - position * rows_here
    owned = (local_pos >= 0) & (local_pos < rows_here)
    row_ids = jnp.arange(rows_here, dtype=jnp.int32)
    selector = owned[:, None] & (local_pos[:, None] == row_ids[None, :])
    projected = jnp.concatenate([query, keys, values], axis=1)
    chosen_rows = jnp.dot(
        selector.astype(jnp.bfloat16), projected, preferred_element_type=jnp.float32
    )
    shared = lax.psum(chosen_rows.astype(jnp.bfloat16), "seq")
    g_query = shared[:, :group_width].reshape(global_count, heads_here, head_size)
    g_key = shared[:, group_width : 2 * group_width].reshape(global_count, heads_here, head_size)
    g_value = shared[:, 2 * group_width :].reshape(global_count, heads_here, head_size)
    global_score_rows = (
        jnp.einsum("bqhd,ghd->bhqg", query_blocks, g_key, preferred_element_type=jnp.float32)
        * score_scale
    )
    top, total, accum, attention_weights = fold_scores(state, global_score_rows, all_valid)
    accum = accum + jnp.einsum(
        "bhqg,ghd->bhqd", attention_weights, g_value, preferred_element_type=jnp.float32
    )
    sparse = (accum / total[..., None]).transpose(0, 2, 1, 3).reshape(rows_here, group_width)
    key_heads = keys.reshape(rows_here, heads_here, head_size)
    value_heads = values.reshape(rows_here, heads_here, head_size)
    g_scores = (
        jnp.einsum("ghd,thd->hgt", g_query, key_heads, preferred_element_type=jnp.float32)
        * score_scale
    )
    g_top = jnp.max(g_scores, axis=-1)
    g_probs = jnp.exp(g_scores - g_top[..., None])
    g_total = jnp.sum(g_probs, axis=-1)
    g_accum = jnp.einsum(
        "hgt,thd->hgd",
        g_probs.astype(jnp.bfloat16),
        value_heads,
        preferred_element_type=jnp.float32,
    )
    merged_top, merged_total, merged_accum = combined_all(
        (g_top, g_total, g_accum), "seq", join_states
    )
    finished = merged_accum / merged_total[..., None]
    placing = selector.astype(jnp.float32).T
    placed = jnp.einsum("tg,hgd->thd", placing, finished, precision=lax.Precision.HIGHEST)
    is_global = jnp.sum(placing, axis=1) > 0.5
    context = jnp.where(is_global[:, None], placed.reshape(rows_here, group_width), sparse).astype(
        jnp.bfloat16
    )
    term = jnp.dot(context, w_out, preferred_element_type=jnp.float32)
    return lax.psum_scatter(term.astype(jnp.bfloat16), "heads", scatter_dimension=1, tiled=True)


def solution(mesh):
    in_specs = (
        P("seq", "heads"),
        P(None, "heads"),
        P(None, "heads"),
        P(None, "heads"),
        P("heads", None),
        P("heads"),
        P("seq", None),
        P(),
    )
    out_specs = P("seq", "heads")
    return jax.shard_map(
        on_device, mesh=mesh, in_specs=in_specs, out_specs=out_specs, check_vma=False
    )
```

profile of v0, /device:TPU:1, one launch (start us, length us, event | category | flops | bytes accessed | tf_op | source)
XLA Modules:
  0.0 761.6 jit_solution(3525437572789591166)
XLA Ops:
  8.0 157.4 %all-gather.9.cloned.1.call-done = bf16[768,4096]{1,0:T(8,128)(2,1)} async-done(((bf16[768,256]{1,0:T(8,128)(2,1)}), bf16[768,4096]{1,0:T(8,128)(2,1)}) %all-gather.9.cloned.1.call-update) | async-done | bytes 6291472 | tf_op jit(solution)/shard_map/all_gather | solution.py:71
  165.4 5.4 convolution_convert_fusion.1
  171.2 2.0 convolution_convert_fusion.2
  173.2 2.0 convolution_convert_fusion.3
  175.2 1.2 fusion.43
  176.5 143.8 %all-reduce.2.cloned.1.call-done = bf16[128,768]{1,0:T(8,128)(2,1)} async-done(((bf16[128,768]{1,0:T(8,128)(2,1)}), bf16[128,768]{1,0:T(8,128)(2,1)}) %all-reduce.2.cloned.1.call-update) | async-done | bytes 196624 | tf_op jit(solution)/shard_map/psum | solution.py:152
  320.3 1.6 fusion.95
  321.9 1.3 fusion.96
  324.3 2.0 pad_maximum_fusion.1
  331.4 1.9 copy.142
  333.4 1.8 reshape.309
  335.2 1.8 fusion.67
  337.5 2.0 collective-permute-start.1
  339.5 26.6 %all-gather.3 = f32[16,2,128]{2,1,0:T(2,128)S(1)} all-gather(f32[1,2,128]{2,1,0:T(2,128)S(1)} %bitcast.208), channel_id=2, replica_groups=mesh['seq'=16,'heads'=16] {'seq'}, dimensions={0}, use_global_device_ids=true | all-gather | bytes 17408 | tf_op jit(solution)/shard_map/all_gather | solution.py:26
  366.4 19.3 %all-gather.4 = f32[16,2,128]{2,1,0:T(2,128)S(1)} all-gather(f32[1,2,128]{2,1,0:T(2,128)S(1)} %bitcast.209), channel_id=3, replica_groups=mesh['seq'=16,'heads'=16] {'seq'}, dimensions={0}, use_global_device_ids=true | all-gather | bytes 17408 | tf_op jit(solution)/shard_map/all_gather | solution.py:26
  386.2 1.6 copy.187
  388.6 2.2 fusion.97
  390.8 2.3 pad_maximum_fusion
  393.1 2.5 copy.143
  395.6 3.0 reshape.310
  402.2 4.7 fusion.94
  406.9 1.8 copy.159
  409.2 2.7 fusion.8
  411.9 3.0 slice.104
  415.0 16.8 %while.14 = (s32[]{:T(128)}, f32[2,128]{1,0:T(2,128)S(1)}, f32[2,128]{1,0:T(2,128)S(1)}, f32[2,128,128]{2,1,0:T(8,128)S(1)}, f32[15,2,128]{2,1,0:T(2,128)S(1)}, ...) while((s32[]{:T(128)}, f32[2,128]{1,0:T(2,128)S(1)}, f32[2,128]{1,0:T(2,128)S(1)}, ...), condition=%wide.region_5.6_spmd, body=%wide.region_4.5_spmd.sunk | while | flops 99842 | bytes 403557 | solution.py:29
  415.0 1.1 fusion.117
  416.1 1.1 fusion.117
  417.2 1.1 fusion.117
  419.5 1.1 fusion.117
  420.6 1.1 fusion.117
  425.0 1.1 fusion.117
  426.2 1.1 fusion.117
  427.4 1.1 fusion.117
  429.6 1.1 fusion.117
  430.7 1.1 fusion.117
  432.0 45.2 %all-gather.11.cloned.1.call-done = bf16[2,12288,256]{1,2,0:T(8,128)(2,1)} async-done(((bf16[2,768,256]{1,2,0:T(8,128)(2,1)}), bf16[2,12288,256]{1,2,0:T(8,128)(2,1)}) %all-gather.11.cloned.1.call-update) | async-done | bytes 12582928 | tf_op jit(solution)/shard_map/all_gather | solution.py:122
  477.2 30.9 %copy.151 = bf16[2,12288,256]{2,0,1:T(2,128)(2,1)} copy(bf16[2,12288,256]{1,2,0:T(8,128)(2,1)} %all-gather.11.cloned.1.call-done) | data formatting | bytes 25165824 | tf_op jit(solution)/shard_map/all_gather | solution.py:122
  508.2 37.2 %gather_fusion.1 = bf16[4096,2,256]{2,1,0:T(2,128)(2,1)} fusion(bf16[2,12288,256]{2,0,1:T(2,128)(2,1)} %copy.151, s32[4096]{0:T(1024)S(1)} %copy-done.8), kind=kCustom, calls=%fused_computation.1 | custom fusion | bytes 8404992 | tf_op jit(solution)/shard_map/gather | solution.py:128
  545.3 9.9 %fusion.93 = (bf16[1,4096,256]{2,0,1:T(2,128)(2,1)}, bf16[1,4096,256]{2,0,1:T(2,128)(2,1)}) fusion(bf16[2,4096,256]{2,0,1:T(2,128)(2,1)} %bitcast.183), kind=kLoop, calls=%fused_computation.149 | loop fusion | bytes 8388608 | tf_op jit(solution)/shard_map/slice | solution.py:131
  555.2 9.8 %copy.152 = bf16[1,4096,256]{1,2,0:T(8,128)(2,1)} copy(bf16[1,4096,256]{2,0,1:T(2,128)(2,1)} %get-tuple-element.72) | data formatting | bytes 4194304 | tf_op jit(solution)/shard_map/slice | solution.py:131
  565.0 9.8 %copy.160 = bf16[1,4096,256]{1,2,0:T(8,128)(2,1)} copy(bf16[1,4096,256]{2,0,1:T(2,128)(2,1)} %get-tuple-element.73) | data formatting | bytes 4194304 | tf_op jit(solution)/shard_map/slice | solution.py:141
  574.8 7.7 %fusion.3 = (f32[6,2,128]{2,0,1:T(8,128)S(1)}, f32[2,4096,6,128]{3,1,2,0:T(8,128)S(1)}) fusion(pred[6,4096]{1,0:T(8,128)(4,1)S(1)} %bitcast.199, bf16[4096,2,128,1]{0,2,3,1:T(8,128)(2,1)} %bitcast.195, bf16[6,128,2,128]{3,2,1,0:T(2,128)(2,1)S(1)} %copy-done.3), kind=kOutput, calls=%fused_computation.13 | convolution fusion | flops 1629485568 | bytes 27686912 | tf_op jit(solution)/shard_map/bqhd,khd->bhqk/dot_general | solution.py:131
  582.7 1.2 fusion.9
  583.9 13.8 %fusion.4 = (f32[6,2,128]{2,0,1:T(8,128)S(1)}, bf16[6,2,128,4096]{2,3,0,1:T(8,128)(2,1)}) fusion(f32[2,4096,6,128]{3,1,2,0:T(8,128)S(1)} %get-tuple-element.89, f32[6,2,128]{2,0,1:T(8,128)S(1)} %copy.162, pred[6,4096]{1,0:T(8,128)(4,1)S(1)} %bitcast.200), kind=kLoop, calls=%fused_computation.14 | loop fusion | flops 37747200 | bytes 37785600 | tf_op jit(solution)/shard_map/reduce_sum | solution.py:41
  597.7 10.6 %fusion.18 = f32[6,128,2,128]{3,1,2,0:T(8,128)} fusion(bf16[4096,2,128,1]{0,2,1,3:T(8,128)(2,1)S(1)} %bitcast.194, bf16[6,2,128,4096]{2,3,0,1:T(8,128)(2,1)} %get-tuple-element.71), kind=kOutput, calls=%fused_computation.31 | convolution fusion | flops 1610612736 | bytes 15466496 | tf_op jit(solution)/shard_map/bhqk,khd->bhqd/dot_general | solution.py:141
  608.3 3.2 fusion.33
  613.0 4.5 convolution_convert_fusion
  617.5 137.5 %reduce-scatter.2.cloned.1.call-done = bf16[768,256]{1,0:T(8,128)(2,1)} async-done(((bf16[768,4096]{1,0:T(8,128)(2,1)}), bf16[768,256]{1,0:T(8,128)(2,1)}) %reduce-scatter.2.cloned.1.call-update) | async-done | bytes 393232 | tf_op jit(solution)/shard_map/reduce_scatter | solution.py:191
  (145 shorter events, 21.9 us)
Async XLA Ops:
  6.5 606.5 %copy-start = (bf16[256,4096]{1,0:T(8,128)(2,1)S(1)}, bf16[256,4096]{1,0:T(8,128)(2,1)}, u32[]{:S(2)}) copy-start(bf16[256,4096]{1,0:T(8,128)(2,1)} %param.14) | copy-start | bytes 6291460
  6.5 158.8 %all-gather.9.cloned.1.call-start = ((), (), s32[]{:S(2)}) async-start(), calls=%async_computation.1 | async-start | bytes 6684672 | tf_op jit(solution)/shard_map/all_gather | solution.py:71
  7.3 313.1 %all-reduce.2.cloned.1.call-start = ((), (), s32[]{:S(2)}) async-start(), calls=%async_computation.2 | async-start | bytes 393216 | tf_op jit(solution)/shard_map/psum | solution.py:152
  8.0 322.1 %copy-start.15 = (pred[128]{0:T(512)(128)(4,1)}, pred[128]{0:T(512)(128)(4,1)S(1)}, u32[]{:S(2)}) copy-start(pred[128]{0:T(512)(128)(4,1)S(1)} %get-tuple-element.68) | copy-start | bytes 388
  8.0 322.1 %copy-start.17 = (s32[128]{0:T(128)}, s32[128]{0:T(128)S(1)}, u32[]{:S(2)}) copy-start(s32[128]{0:T(128)S(1)} %get-tuple-element.69) | copy-start | bytes 1540
  165.4 5.4 copy-start.20
  165.4 5.8 copy-start.21
  171.2 2.0 copy-start.22
  173.2 2.0 copy-start.2
  175.2 146.7 %copy-start.6 = (bf16[768,256]{0,1:T(8,128)(2,1)}, bf16[768,256]{0,1:T(8,128)(2,1)S(1)}, u32[]{:S(2)}) copy-start(bf16[768,256]{0,1:T(8,128)(2,1)S(1)} %convolution_convert_fusion.3) | copy-start | bytes 1179652
  175.2 151.2 %copy-start.23 = (s32[2]{0:T(128)S(1)}, s32[2]{0:T(128)}, u32[]{:S(2)}) copy-start(s32[2]{0:T(128)} %param.15) | copy-start | bytes 28
  175.2 151.9 %copy-start.14 = (s32[6,3]{0,1:T(4,128)S(1)}, s32[6,3]{0,1:T(4,128)}, u32[]{:S(2)}) copy-start(s32[6,3]{0,1:T(4,128)} %param.16) | copy-start | bytes 220
  176.5 235.4 %all-gather.13.cloned.1.call-start = ((), (), s32[]{:S(2)}) async-start(), calls=%async_computation.5 | async-start | bytes 2228224 | tf_op jit(solution)/shard_map/all_gather | solution.py:26
  324.3 152.9 %all-gather.11.cloned.1.call-start = ((), (), s32[]{:S(2)}) async-start(), calls=%async_computation.3 | async-start | bytes 13369344 | tf_op jit(solution)/shard_map/all_gather | solution.py:122
  326.3 428.7 %reduce-scatter.2.cloned.1.call-start = ((), (), s32[]{:S(2)}) async-start(), calls=%async_computation.4 | async-start | bytes 6684672 | tf_op jit(solution)/shard_map/reduce_scatter | solution.py:191
  337.0 53.8 %collective-permute-start = (bf16[2,256,256]{1,2,0:T(8,128)(2,1)}, bf16[2,256,256]{1,2,0:T(8,128)(2,1)S(1)}, u32[]{:S(2)}, u32[]{:S(2)}) collective-permute-start(bf16[2,256,256]{1,2,0:T(8,128)(2,1)} %get-tuple-element.78), channel_id=1, source_target_pairs={{0,16},{16,32},{32,48},{48,64},{64,80},{80,96},{96,112},{112,128},... | collective-permute-start | bytes 786440 | tf_op jit(solution)/shard_map/ppermute | solution.py:17
  337.5 53.3 %collective-permute-start.1 = (bf16[2,256,256]{1,2,0:T(8,128)(2,1)}, bf16[2,256,256]{1,2,0:T(8,128)(2,1)}, u32[]{:S(2)}, u32[]{:S(2)}) collective-permute-start(bf16[2,256,256]{1,2,0:T(8,128)(2,1)} %get-tuple-element.79), channel_id=1, source_target_pairs={{16,0},{32,16},{48,32},{64,48},{80,64},{96,80},{112,96},{128,112},... | collective-permute-start | bytes 786440 | tf_op jit(solution)/shard_map/ppermute | solution.py:20
  366.1 20.1 %copy-start.10 = (f32[16,2,128]{2,1,0:T(2,128)}, f32[16,2,128]{2,1,0:T(2,128)S(1)}, u32[]{:S(2)}) copy-start(f32[16,2,128]{2,1,0:T(2,128)S(1)} %all-gather.3) | copy-start | bytes 49156
  385.6 0.6 copy-start.11
  406.8 2.3 copy-start.3
  406.8 2.3 copy-start.13
  409.2 5.8 slice-start.1
  409.2 5.8 slice-start.2
  409.2 5.8 copy-start.12
  411.9 3.1 slice-start
  432.0 76.1 %copy-start.8 = (s32[4096]{0:T(1024)S(1)}, s32[4096]{0:T(1024)}, u32[]{:S(2)}) copy-start(s32[4096]{0:T(1024)} %broadcast_clamp_fusion) | copy-start | bytes 49156
  565.0 9.8 %copy-start.7 = (pred[1,6,32,128]{3,1,2,0:T(8,128)(4,1)S(1)}, pred[1,6,32,128]{3,1,2,0:T(8,128)(4,1)}, u32[]{:S(2)}) copy-start(pred[1,6,32,128]{3,1,2,0:T(8,128)(4,1)} %copy.235) | copy-start | bytes 73732
  574.8 7.8 %copy-start.4 = (f32[6,2,128,128]{2,3,0,1:T(8,128)S(1)}, f32[6,2,128,128]{2,3,0,1:T(8,128)}, u32[]{:S(2)}) copy-start(f32[6,2,128,128]{2,3,0,1:T(8,128)} %get-tuple-element.87) | copy-start | bytes 2359300
  574.8 7.9 %copy-start.1 = (f32[6,2,128,640]{3,2,1,0:T(8,128)S(1)}, f32[6,2,128,640]{3,2,1,0:T(8,128)}, u32[]{:S(2)}) copy-start(f32[6,2,128,640]{3,2,1,0:T(8,128)} %get-tuple-element.91) | copy-start | bytes 11796484
  583.9 13.8 %copy-start.5 = (bf16[1,4096,256]{1,2,0:T(8,128)(2,1)S(1)}, bf16[1,4096,256]{1,2,0:T(8,128)(2,1)}, u32[]{:S(2)}) copy-start(bf16[1,4096,256]{1,2,0:T(8,128)(2,1)} %copy.160) | copy-start | bytes 6291460
  608.3 3.2 copy-start.9
  611.5 0.9 copy-start.16
  611.5 0.9 copy-start.18
  611.5 0.9 copy-start.19
Sparse Core Ops, SparseCore 0:
  9.1 156.2 all-gather.8
  176.6 143.6 all-reduce.1
  324.4 55.9 all-gather.12
  383.3 93.8 all-gather.10
  617.7 137.3 reduce-scatter.1
where the time goes:
time: 764 us; the launch traced here: 762 us
  waiting for transfers between devices  485 us (63%)
  local copies, waits for them, and re-layouts  129 us (17%)
  blocking collectives  45.8 us (6%)
  matrix products  44.8 us (6%)
  other arithmetic  40.8 us (5%)
  between operations  13.7 us (2%)
    all_gather x1, waiting for transfers between devices, on_device(): piece = lax.all_gather(activations, 'heads', axis=1, tiled=True)  157 us
    psum x1, waiting for transfers between devices, on_device(): shared = lax.psum(chosen_rows.astype(jnp.bfloat16), 'seq')  144 us
    reduce_scatter x1, waiting for transfers between devices, on_device(): lax.psum_scatter(term.astype(jnp.bfloat16), 'heads', scatter_dimension=1,...  137 us
    all_gather x2, blocking collectives, combined_all(): pieces = jax.tree.map(lambda part: lax.all_gather(part, axis), value)  45.8 us
    all_gather x1, waiting for transfers between devices, on_device(): piece = lax.all_gather(stacked, 'seq', axis=1, tiled=True)  45.2 us
    gather x1, local copies, waits for them, and re-layouts, on_device(): chosen = piece[:, jnp.clip(offset_rows, 0, count - 1).reshape(-1)]  37.2 us
    all_gather x1, local copies, waits for them, and re-layouts, on_device(): piece = lax.all_gather(stacked, 'seq', axis=1, tiled=True)  30.9 us
    slice x2, local copies, waits for them, and re-layouts, on_device(): chosen[0]  19.7 us
  transfers between devices with their start and end apart: 7, of which 4 were waited for; matrix products, arithmetic and copies ran while one was open for 8% of the time, Pallas kernels for 0%

commit v1 on v0

--- a/solution.py
+++ b/solution.py
@@ -3,6 +3,7 @@
 import jax.numpy as jnp
 from jax import lax
 from jax.sharding import PartitionSpec as P
+from jax.lax import all_gather
 
 WMAX = 2
 NEGATIVE = -1e30
@@ -149,7 +150,8 @@
     chosen_rows = jnp.dot(
         selector.astype(jnp.bfloat16), projected, preferred_element_type=jnp.float32
     )
-    shared = lax.psum(chosen_rows.astype(jnp.bfloat16), "seq")
+    incoming_x = chosen_rows.astype(jnp.bfloat16)
+    shared = jnp.sum(all_gather(incoming_x, axis_name="seq"), axis=0)
     g_query = shared[:, :group_width].reshape(global_count, heads_here, head_size)
     g_key = shared[:, group_width : 2 * group_width].reshape(global_count, heads_here, head_size)
     g_value = shared[:, 2 * group_width :].reshape(global_count, heads_here, head_size)

time: 764 us -> 681 us (0.89)
  waiting for transfers between devices: 485 us -> 411 us
    psum x1 -> x0, waiting for transfers between devices: 144 us -> none  [on_device(): shared = lax.psum(chosen_rows.astype(jnp.bfloat16), 'seq')]
    all_gather x0 -> x1, waiting for transfers between devices: none -> 63.6 us  [on_device(): shared = jnp.sum(all_gather(incoming_x, axis_name='seq'), axis=0)]
  transfers between devices with their start and end apart: 7 -> 7, of which waited for: 4 -> 6; matrix products, arithmetic and copies ran while one was open for 8% -> 8% of each run, Pallas kernels for 0% -> 0%
where the time goes in v1:
time: 681 us; the launch traced here: 679 us
  waiting for transfers between devices  411 us (60%)
  local copies, waits for them, and re-layouts  125 us (18%)
  blocking collectives  44.1 us (6%)
  matrix products  42.9 us (6%)
  other arithmetic  40.7 us (6%)
  between operations  13.6 us (2%)
    all_gather x1, waiting for transfers between devices, on_device(): piece = lax.all_gather(activations, 'heads', axis=1, tiled=True)  157 us
    reduce_scatter x1, waiting for transfers between devices, on_device(): lax.psum_scatter(term.astype(jnp.bfloat16), 'heads', scatter_dimension=1,...  138 us
    all_gather x1, waiting for transfers between devices, on_device(): shared = jnp.sum(all_gather(incoming_x, axis_name='seq'), axis=0)  63.6 us
    all_gather x1, waiting for transfers between devices, on_device(): piece = lax.all_gather(stacked, 'seq', axis=1, tiled=True)  48.9 us
    all_gather x2, blocking collectives, combined_all(): pieces = jax.tree.map(lambda part: lax.all_gather(part, axis), value)  44.1 us
    gather x1, local copies, waits for them, and re-layouts, on_device(): chosen = piece[:, jnp.clip(offset_rows, 0, count - 1).reshape(-1)]  37.2 us
    all_gather x1, local copies, waits for them, and re-layouts, on_device(): piece = lax.all_gather(stacked, 'seq', axis=1, tiled=True)  30.9 us
    slice x2, local copies, waits for them, and re-layouts, on_device(): chosen[0]  19.8 us
  transfers between devices with their start and end apart: 7, of which 6 were waited for; matrix products, arithmetic and copies ran while one was open for 8% of the time, Pallas kernels for 0%

profile of v1, /device:TPU:1, one launch (start us, length us, event | category | flops | bytes accessed | tf_op | source)
XLA Modules:
  0.0 678.6 jit_solution(6983713132792704041)
XLA Ops:
  8.0 157.4 %all-gather.11.cloned.1.call-done = bf16[768,4096]{1,0:T(8,128)(2,1)} async-done(((bf16[768,256]{1,0:T(8,128)(2,1)}), bf16[768,4096]{1,0:T(8,128)(2,1)}) %all-gather.11.cloned.1.call-update) | async-done | bytes 6291472 | tf_op jit(solution)/shard_map/all_gather | solution.py:72
  165.4 5.4 convolution_convert_fusion.1
  171.2 2.0 convolution_convert_fusion.2
  173.2 2.0 convolution_convert_fusion.3
  175.9 1.2 fusion.43
  177.2 63.6 %all-gather.15.cloned.1.call-done = bf16[2048,768]{1,0:T(8,128)(2,1)} async-done(((bf16[128,768]{1,0:T(8,128)(2,1)}), bf16[2048,768]{1,0:T(8,128)(2,1)}) %all-gather.15.cloned.1.call-update) | async-done | bytes 3145744 | tf_op jit(solution)/shard_map/all_gather | solution.py:154
  240.9 2.3 reduce_sum.82
  253.9 1.2 copy.142
  256.2 2.7 collective-permute-done.1
  258.8 2.1 pad_maximum_fusion
  261.0 2.4 copy.143
  263.4 3.0 reshape.310
  270.0 4.7 fusion.91
  274.7 1.8 copy.160
  277.0 2.7 fusion.8
  280.2 24.4 %all-gather.5 = f32[16,2,128]{2,1,0:T(2,128)S(1)} all-gather(f32[1,2,128]{2,1,0:T(2,128)S(1)} %bitcast.212), channel_id=4, replica_groups=mesh['seq'=16,'heads'=16] {'seq'}, dimensions={0}, use_global_device_ids=true | all-gather | bytes 17408 | tf_op jit(solution)/shard_map/all_gather | solution.py:27
  304.7 19.6 %all-gather.4 = f32[16,2,128]{2,1,0:T(2,128)S(1)} all-gather(f32[1,2,128]{2,1,0:T(2,128)S(1)} %bitcast.211), channel_id=3, replica_groups=mesh['seq'=16,'heads'=16] {'seq'}, dimensions={0}, use_global_device_ids=true | all-gather | bytes 17408 | tf_op jit(solution)/shard_map/all_gather | solution.py:27
  324.3 1.2 fusion.94
  325.5 3.1 slice.104
  328.6 16.8 %while.14 = (s32[]{:T(128)}, f32[2,128]{1,0:T(2,128)S(1)}, f32[2,128]{1,0:T(2,128)S(1)}, f32[2,128,128]{2,1,0:T(8,128)S(1)}, f32[15,2,128]{2,1,0:T(2,128)S(1)}, ...) while((s32[]{:T(128)}, f32[2,128]{1,0:T(2,128)S(1)}, f32[2,128]{1,0:T(2,128)S(1)}, ...), condition=%wide.region_5.6_spmd, body=%wide.region_4.5_spmd.sunk | while | flops 99842 | bytes 403557 | solution.py:30
  328.6 1.1 fusion.116
  329.7 1.1 fusion.116
  330.8 1.1 fusion.116
  331.9 1.1 fusion.116
  333.1 1.1 fusion.116
  334.2 1.1 fusion.116
  335.3 1.1 fusion.116
  336.4 1.1 fusion.116
  337.5 1.1 fusion.116
  338.6 1.1 fusion.116
  339.8 1.1 fusion.116
  340.9 1.1 fusion.116
  342.0 1.1 fusion.116
  343.1 1.1 fusion.116
  344.3 1.1 fusion.116
  345.6 48.9 %all-gather.13.cloned.1.call-done = bf16[2,12288,256]{1,2,0:T(8,128)(2,1)} async-done(((bf16[2,768,256]{1,2,0:T(8,128)(2,1)}), bf16[2,12288,256]{1,2,0:T(8,128)(2,1)}) %all-gather.13.cloned.1.call-update) | async-done | bytes 12582928 | tf_op jit(solution)/shard_map/all_gather | solution.py:123
  394.5 30.9 %copy.151 = bf16[2,12288,256]{2,0,1:T(2,128)(2,1)} copy(bf16[2,12288,256]{1,2,0:T(8,128)(2,1)} %all-gather.13.cloned.1.call-done) | data formatting | bytes 25165824 | tf_op jit(solution)/shard_map/all_gather | solution.py:123
  425.4 37.2 %gather_fusion.1 = bf16[4096,2,256]{2,1,0:T(2,128)(2,1)} fusion(bf16[2,12288,256]{2,0,1:T(2,128)(2,1)} %copy.151, s32[4096]{0:T(1024)S(1)} %copy-done.11), kind=kCustom, calls=%fused_computation.1 | custom fusion | bytes 8404992 | tf_op jit(solution)/shard_map/gather | solution.py:129
  462.6 10.1 %fusion.90 = (bf16[1,4096,256]{2,0,1:T(2,128)(2,1)}, bf16[1,4096,256]{2,0,1:T(2,128)(2,1)}) fusion(bf16[2,4096,256]{2,0,1:T(2,128)(2,1)} %bitcast.184), kind=kLoop, calls=%fused_computation.145 | loop fusion | bytes 8388608 | tf_op jit(solution)/shard_map/slice | solution.py:132
  472.6 9.8 %copy.152 = bf16[1,4096,256]{1,2,0:T(8,128)(2,1)} copy(bf16[1,4096,256]{2,0,1:T(2,128)(2,1)} %get-tuple-element.72) | data formatting | bytes 4194304 | tf_op jit(solution)/shard_map/slice | solution.py:132
  482.4 9.8 %copy.161 = bf16[1,4096,256]{1,2,0:T(8,128)(2,1)} copy(bf16[1,4096,256]{2,0,1:T(2,128)(2,1)} %get-tuple-element.73) | data formatting | bytes 4194304 | tf_op jit(solution)/shard_map/slice | solution.py:142
  492.2 7.7 %fusion.3 = (f32[6,2,128]{2,0,1:T(8,128)S(1)}, f32[2,4096,6,128]{3,1,2,0:T(8,128)S(1)}) fusion(pred[6,4096]{1,0:T(8,128)(4,1)S(1)} %bitcast.202, bf16[4096,2,128,1]{0,2,3,1:T(8,128)(2,1)} %bitcast.197, bf16[6,128,2,128]{3,2,1,0:T(2,128)(2,1)S(1)} %copy-done.4), kind=kOutput, calls=%fused_computation.13 | convolution fusion | flops 1629485568 | bytes 27686912 | tf_op jit(solution)/shard_map/bqhd,khd->bhqk/dot_general | solution.py:132
  500.1 1.2 fusion.9
  501.3 13.5 %fusion.4 = (f32[6,2,128]{2,0,1:T(8,128)S(1)}, bf16[6,2,128,4096]{2,3,0,1:T(8,128)(2,1)}) fusion(f32[2,4096,6,128]{3,1,2,0:T(8,128)S(1)} %get-tuple-element.89, f32[6,2,128]{2,0,1:T(8,128)S(1)} %copy.163, pred[6,4096]{1,0:T(8,128)(4,1)S(1)} %bitcast.203), kind=kLoop, calls=%fused_computation.14 | loop fusion | flops 37747200 | bytes 37785600 | tf_op jit(solution)/shard_map/reduce_sum | solution.py:42
  514.8 10.6 %fusion.18 = f32[6,128,2,128]{3,1,2,0:T(8,128)} fusion(bf16[4096,2,128,1]{0,2,1,3:T(8,128)(2,1)S(1)} %bitcast.196, bf16[6,2,128,4096]{2,3,0,1:T(8,128)(2,1)} %get-tuple-element.71), kind=kOutput, calls=%fused_computation.31 | convolution fusion | flops 1610612736 | bytes 15466496 | tf_op jit(solution)/shard_map/bhqk,khd->bhqd/dot_general | solution.py:142
  525.4 3.2 fusion.33
  530.1 4.5 convolution_convert_fusion
  534.6 137.5 %reduce-scatter.2.cloned.1.call-done = bf16[768,256]{1,0:T(8,128)(2,1)} async-done(((bf16[768,4096]{1,0:T(8,128)(2,1)}), bf16[768,256]{1,0:T(8,128)(2,1)}) %reduce-scatter.2.cloned.1.call-update) | async-done | bytes 393232 | tf_op jit(solution)/shard_map/reduce_scatter | solution.py:193
  (137 shorter events, 21.0 us)
Async XLA Ops:
  6.5 523.5 %copy-start = (bf16[256,4096]{1,0:T(8,128)(2,1)S(1)}, bf16[256,4096]{1,0:T(8,128)(2,1)}, u32[]{:S(2)}) copy-start(bf16[256,4096]{1,0:T(8,128)(2,1)} %param.14) | copy-start | bytes 6291460
  6.5 158.8 %all-gather.11.cloned.1.call-start = ((), (), s32[]{:S(2)}) async-start(), calls=%async_computation.1 | async-start | bytes 6684672 | tf_op jit(solution)/shard_map/all_gather | solution.py:72
  7.3 233.6 %all-gather.15.cloned.1.call-start = ((), (), s32[]{:S(2)}) async-start(), calls=%async_computation.4 | async-start | bytes 3342336 | tf_op jit(solution)/shard_map/all_gather | solution.py:154
  8.0 241.7 %copy-start.13 = (s32[128]{0:T(128)}, s32[128]{0:T(128)S(1)}, u32[]{:S(2)}) copy-start(s32[128]{0:T(128)S(1)} %get-tuple-element.69) | copy-start | bytes 1540
  165.4 5.4 copy-start.16
  165.4 5.8 copy-start.17
  171.2 2.0 copy-start.18
  175.2 0.7 copy-start.7
  177.2 148.3 %all-gather.17.cloned.1.call-start = ((), (), s32[]{:S(2)}) async-start(), calls=%async_computation.5 | async-start | bytes 2228224 | tf_op jit(solution)/shard_map/all_gather | solution.py:27
  240.9 6.6 copy-start.12
  243.2 6.6 copy-start.19
  244.4 0.9 copy-start.2
  246.4 148.1 %all-gather.13.cloned.1.call-start = ((), (), s32[]{:S(2)}) async-start(), calls=%async_computation.2 | async-start | bytes 13369344 | tf_op jit(solution)/shard_map/all_gather | solution.py:123
  247.4 424.7 %reduce-scatter.2.cloned.1.call-start = ((), (), s32[]{:S(2)}) async-start(), calls=%async_computation.3 | async-start | bytes 6684672 | tf_op jit(solution)/shard_map/reduce_scatter | solution.py:193
  251.5 4.7 collective-permute-start
  252.5 6.3 collective-permute-start.1
  274.6 2.4 copy-start.4
  277.0 2.8 copy-start.9
  277.0 2.9 copy-start.8
  277.0 3.0 copy-start.3
  325.5 3.1 slice-start
  345.6 79.8 %copy-start.11 = (s32[4096]{0:T(1024)S(1)}, s32[4096]{0:T(1024)}, u32[]{:S(2)}) copy-start(s32[4096]{0:T(1024)} %broadcast_clamp_fusion) | copy-start | bytes 49156
  482.4 9.8 %copy-start.10 = (pred[1,6,32,128]{3,1,2,0:T(8,128)(4,1)S(1)}, pred[1,6,32,128]{3,1,2,0:T(8,128)(4,1)}, u32[]{:S(2)}) copy-start(pred[1,6,32,128]{3,1,2,0:T(8,128)(4,1)} %copy.225) | copy-start | bytes 73732
  492.2 7.7 %copy-start.5 = (f32[6,2,128,128]{2,3,0,1:T(8,128)S(1)}, f32[6,2,128,128]{2,3,0,1:T(8,128)}, u32[]{:S(2)}) copy-start(f32[6,2,128,128]{2,3,0,1:T(8,128)} %get-tuple-element.87) | copy-start | bytes 2359300
  492.2 7.9 %copy-start.1 = (f32[6,2,128,640]{3,2,1,0:T(8,128)S(1)}, f32[6,2,128,640]{3,2,1,0:T(8,128)}, u32[]{:S(2)}) copy-start(f32[6,2,128,640]{3,2,1,0:T(8,128)} %get-tuple-element.91) | copy-start | bytes 11796484
  501.3 13.5 %copy-start.6 = (bf16[1,4096,256]{1,2,0:T(8,128)(2,1)S(1)}, bf16[1,4096,256]{1,2,0:T(8,128)(2,1)}, u32[]{:S(2)}) copy-start(bf16[1,4096,256]{1,2,0:T(8,128)(2,1)} %copy.161) | copy-start | bytes 6291460
  528.6 0.9 copy-start.14
  528.6 0.9 copy-start.15
Sparse Core Ops, SparseCore 0:
  9.1 156.2 all-gather.10
  177.3 63.5 all-gather.14
  246.5 51.4 all-gather.16
  300.6 93.8 all-gather.12
  534.7 137.3 reduce-scatter.1
